TPU v7x, 768 devices: a whole 4x8x12 slice. The times are simulated.
768 devices in a mesh: pw: 16 (over y, core), band: 48 (over x, z).
Axes of the slice: x: 4, y: 8, z: 12, core: 2. Of those that a mesh axis runs over, the one named last changes fastest.
Arguments:
- psi: bfloat16 [2, 48, 98304], P(None, 'band', 'pw'), may hold values from -9 to 9
- gvec_index: int32 [98304], P('pw'), may hold values from 0 to 442367, as said below
- vloc: float32 [192, 192, 192], P(None, 'pw'), may hold values from -3 to 1
- beta: bfloat16 [2, 72, 98304], P(None, None, 'pw'), may hold values from -0.078125 to 0.078125
- dmat: float32 [4, 18, 18], replicated, may hold values from -1 to 3
- qmat: float32 [4, 18, 18], replicated, may hold values from -1 to 2
Outputs:
- hpsi: bfloat16 [2, 48, 98304], P(None, 'band', 'pw')
- spsi: bfloat16 [2, 48, 98304], P(None, 'band', 'pw')
- gram: float32 [2, 48, 48], P(None, 'band')
Inputs may be any that keep to these rules, and one draw needn't show every extreme that they name: `gvec_index`: each entry is (x - k * 12) * 192 * 192 + y * 192 + z for the grid cell (x, y, z) of its plane wave, where k is the entry's block of 6144 plane waves and x lies in k * 12 .. (k + 1) * 12 - 1; no cell appears twice.
All inputs are finite; a program needn't handle non-finite values.
Results may differ from a plain program's by a relative error of at most 0.0069.
Values may be sent and summed in bfloat16 or wider, within the bound.
A program may use at most 64 MiB of HBM per device.

v0:
```python
import numpy as np
import jax, jax.numpy as jnp
from jax import lax
from jax.experimental import pallas as pl
from jax.experimental.pallas import tpu as pltpu
from jax.sharding import PartitionSpec as P

NG = 192
KD = 12
F32, BF16 = jnp.float32, jnp.bfloat16
TWO_PI = 2.0 * np.pi
CH = 24
CHB = 16


def dft_tables():
    j = np.arange(NG)
    ang = (j[:, None] * j[None, :] % NG).astype(np.float32) * np.float32(TWO_PI / NG)
    fac = np.float32(1.0) / np.sqrt(np.float32(NG))
    c = np.cos(ang).astype(np.float32) * fac
    s = np.sin(ang).astype(np.float32) * fac
    def zt(sign):
        t = np.zeros((512, 512), np.float32)
        t[:NG, :NG] = c; t[256:256 + NG, 256:256 + NG] = c
        t[:NG, 256:256 + NG] = sign * s; t[256:256 + NG, :NG] = -sign * s
        return t
    pad = (np.arange(NG) // KD) * 16 + np.arange(NG) % KD
    def xt(sign):
        t = np.zeros((2 * NG, 512), np.float32)
        t[:NG, pad] = c; t[NG:, 256 + pad] = c
        t[:NG, 256 + pad] = -sign * s; t[NG:, pad] = sign * s
        return t
    b = lambda t: np.asarray(t, dtype=jnp.bfloat16)
    return b(zt(1.0)), b(zt(-1.0)), b(xt(1.0)), b(xt(1.0).T)


def mod_floor(v, m):
    return v - m * jnp.floor((v + 0.5) * (1.0 / m))


def turn(t):
    h = t * np.float32(np.pi)
    q = h * h
    s = h * (1.0 + q * (-1 / 6 + q * (1 / 120 + q * (-1 / 5040 + q * (1 / 362880 + q * (-1 / 39916800))))))
    c = 1.0 + q * (-1 / 2 + q * (1 / 24 + q * (-1 / 720 + q * (1 / 40320 + q * (-1 / 3628800 + q * (1 / 479001600))))))
    return 1.0 - 2.0 * s * s, 2.0 * s * c


def split_index(idx):
    v = idx.astype(F32)
    x = jnp.floor((v + 0.5) * (1.0 / (NG * NG)))
    r = v - x * (NG * NG)
    y = jnp.floor((r + 0.5) * (1.0 / NG))
    return x, y, r - y * NG


def phases(y, p):
    fac = np.float32(1.0) / np.sqrt(np.float32(NG))
    m = mod_floor(y * p.astype(F32), 16.0)
    ar, ai = turn(jnp.where(m > 8.0, m - 16.0, m) * (1.0 / 16.0))
    wr, wi = turn(jnp.where(y > 96.0, y - 192.0, y) * np.float32(1.0 / NG))
    out = []
    for j in range(KD):
        out.append(((ar * fac).astype(BF16).astype(F32), (ai * fac).astype(BF16).astype(F32)))
        if j < KD - 1:
            ar, ai = ar * wr - ai * wi, ar * wi + ai * wr
    return out


def prep_index(idx, p, li_ref):
    x, y, z = split_index(idx)
    w = x * NG + z
    hi = jnp.floor((w + 0.5) * (1.0 / 256.0))
    li_ref[:, 0, :] = w - hi * 256.0
    li_ref[:, 1, :] = hi
    return phases(y, p)


def one_hot(li_ref, t, n):
    rows = lax.broadcasted_iota(jnp.int32, (256, 128), 0).astype(F32).astype(BF16)
    parts = []
    for k in range(n):
        lo = li_ref[t + k, 0:1, :].astype(BF16)
        parts.append(jnp.where(rows == lo, jnp.array(1, BF16), jnp.array(0, BF16)))
    return jnp.concatenate(parts, axis=1) if n > 1 else parts[0]


def spread(v_ref, li_ref, t, n):
    upper = (lax.broadcasted_iota(jnp.int32, (48, 128), 0) >= 24).astype(F32)
    cols = []
    for k in range(n):
        v = v_ref[t + k]
        v = jnp.concatenate([v, v], axis=0).astype(BF16)
        h = (li_ref[t + k, 1:2, :] - upper).astype(BF16)
        zero = jnp.zeros_like(v)
        rows = [jnp.where(h == jnp.array(2 * q, BF16), v, zero) for q in range(4)]
        rows.append(jnp.where(h == jnp.array(8, BF16), v, zero)[:24])
        cols.append(jnp.concatenate(rows, axis=0))
    return jnp.concatenate(cols, axis=1) if n > 1 else cols[0]


def forward_block(psi, idx, p, base, f_ref, v_ref, li_ref, acc_ref, ch):
    e = prep_index(idx, p, li_ref)
    pr, pi = psi[0].astype(F32), psi[1].astype(F32)
    for j in range(KD):
        er, ei = e[j]
        v_ref[:, j, :] = pr * er - pi * ei
        v_ref[:, KD + j, :] = pr * ei + pi * er
    acc_ref[...] = jnp.zeros_like(acc_ref)

    def step(i, carry):
        t = i * ch
        zt = one_hot(li_ref, t, ch)
        l = spread(v_ref, li_ref, t, ch)
        acc_ref[...] += lax.dot_general(l, zt, (((1,), (1,)), ((), ())), preferred_element_type=F32)
        return carry
    lax.fori_loop(0, 48 // ch, step, 0)
    left = lax.broadcasted_iota(jnp.int32, (24, 128), 1) < 64
    for g in range(3):
        a = [[acc_ref[(3 * g + h) * 24:(3 * g + h + 1) * 24, 128 * q:128 * (q + 1)] for q in range(2)] for h in range(3)]
        r01, r10 = pltpu.roll(a[0][1], 64, 1), pltpu.roll(a[1][0], 64, 1)
        r20, r21 = pltpu.roll(a[2][0], 64, 1), pltpu.roll(a[2][1], 64, 1)
        pieces = [(a[0][0], a[0][1]), (jnp.where(left, r01, r10), r10), (a[1][1], a[2][0]), (jnp.where(left, r20, r21), r21)]
        for k, (low, high) in enumerate(pieces):
            f_ref[base, :, 4 * g + k, 0:128] = low
            f_ref[base, :, 4 * g + k, 128:256] = high
    f_ref[base, :, KD:16, :] = jnp.zeros((24, 16 - KD, 256), F32)


def dense_plane(j, f_ref, vloc_ref, zp, zm, xp, xm):
    dot = lambda a, b: jnp.dot(a, b, preferred_element_type=F32)
    fr, fi = (f_ref[:, c * KD + j].reshape(256, 256).astype(BF16) for c in range(2))
    y = dot(jnp.concatenate([fr, fi], axis=1), zp[...]).astype(BF16)
    y = jnp.concatenate([y[:, 0:NG], y[:, 256:256 + NG]], axis=0)
    s = dot(xp[...], y)
    v = vloc_ref[j]
    s = jnp.concatenate([s[:NG] * v, s[NG:] * v], axis=0).astype(BF16)
    s = dot(xm[...], s).astype(BF16)
    out = dot(s[:256], zm[0:NG, :]) + dot(s[256:], zm[256:256 + NG, :])
    f_ref[:, j] = out[:, :256].reshape(16, 16, 256)
    f_ref[:, KD + j] = out[:, 256:].reshape(16, 16, 256)


def backward_block(idx, p, base, f_ref, e_ref, li_ref, b_ref, s_ref, ch):
    e = prep_index(idx, p, li_ref)
    for j in range(KD):
        er, ei = e[j]
        e_ref[:, j, :] = er
        e_ref[:, KD + j, :] = ei
        e_ref[:, 2 * KD + j, :] = -ei
        e_ref[:, 3 * KD + j, :] = er
    left = lax.broadcasted_iota(jnp.int32, (24, 128), 1) < 64
    for g in range(3):
        x = []
        for k in range(4):
            x.append([f_ref[base, :, 4 * g + k, 128 * q:128 * (q + 1)] for q in range(2)])
        r10, r11 = pltpu.roll(x[1][0], 64, 1), pltpu.roll(x[1][1], 64, 1)
        r30, r31 = pltpu.roll(x[3][0], 64, 1), pltpu.roll(x[3][1], 64, 1)
        pieces = [(x[0][0], jnp.where(left, x[0][1], r10)), (jnp.where(left, r10, r11), x[2][0]),
                  (jnp.where(left, x[2][1], r30), jnp.where(left, r30, r31))]
        for h, (low, high) in enumerate(pieces):
            r = (3 * g + h) * 24
            b_ref[r:r + 24, 0:128] = low
            b_ref[r:r + 24, 128:256] = high

    bm = b_ref[...].astype(BF16)

    def step(i, carry):
        t = i * ch
        tt = jnp.dot(bm, one_hot(li_ref, t, ch), preferred_element_type=F32)
        for k in range(ch):
            hi = jnp.broadcast_to(li_ref[t + k, 1:2, :], (24, 128))
            sel = tt[0:24, 128 * k:128 * (k + 1)]
            for h in range(1, 9):
                sel = jnp.where(hi == float(h), tt[24 * h:24 * (h + 1), 128 * k:128 * (k + 1)], sel)
            ev = e_ref[t + k]
            a, b = sel * ev[:24], sel * ev[24:]
            s_ref[0, t + k] = a[0:8] + a[8:16] + a[16:24]
            s_ref[1, t + k] = b[0:8] + b[8:16] + b[16:24]
        return carry
    lax.fori_loop(0, 48 // ch, step, 0)
    re, im = s_ref[0, :, 0, :], s_ref[1, :, 0, :]
    for k in range(1, 8):
        re = re + s_ref[0, :, k, :]
        im = im + s_ref[1, :, k, :]
    return re, im


N_BAND = 48
N_PW = 16


def pw_peer(p, s):
    k = lax.div(s, 2)
    dy = lax.div(k + 1, 2) * (2 * lax.rem(k, 2) - 1)
    y = lax.rem(lax.div(p, 2) + dy + 8, 8)
    return 2 * y + lax.rem(p + s, 2)


def kernel(psi_ref, idx_ref, vloc_ref, beta_ref, bd_ref, zp, zm, xp, xm, h_ref, s_out, g_out,
           f_ref, v_ref, li_ref, acc_ref, e_ref, b_ref, s_ref, nl_ref, loc_ref, pr_ref,
           ag_psi, ag_idx, pj_send, pj_recv, cf, gb, m_ref, rb, q_send, qb, gs, gr, ls, lr,
           agp_s, agp_r, agi_s, agi_r, pj_s, pj_r, gb_s, gb_r, rb_s, rb_r, q_s, q_r, gr_s, gr_r, ls_s, lr_r):
    p, b = lax.axis_index("pw"), lax.axis_index("band")

    def band_peer(s):
        return lax.rem(b + s, N_BAND)

    def copy_pw(src, dst, ssem, rsem, peer, slot):
        return pltpu.make_async_remote_copy(src_ref=src, dst_ref=dst.at[slot], send_sem=ssem.at[peer],
                                            recv_sem=rsem.at[slot], device_id={"pw": peer},
                                            device_id_type=pl.DeviceIdType.MESH)

    def copy_band(src, dst, ssem, rsem, peer, slot):
        return pltpu.make_async_remote_copy(src_ref=src, dst_ref=dst.at[slot], send_sem=ssem.at[peer],
                                            recv_sem=rsem.at[slot], device_id={"band": peer},
                                            device_id_type=pl.DeviceIdType.MESH)

    def each(first, last, body):
        def step(s, carry):
            body(s)
            return carry
        lax.fori_loop(first, last, step, 0)

    barrier = pltpu.get_barrier_semaphore()
    each(1, N_PW, lambda s: pl.semaphore_signal(barrier, inc=1, device_id={"pw": pw_peer(p, s)},
                                                device_id_type=pl.DeviceIdType.MESH))
    each(1, N_BAND, lambda s: pl.semaphore_signal(barrier, inc=1, device_id={"band": band_peer(s)},
                                                  device_id_type=pl.DeviceIdType.MESH))

    for t in range(48):
        cf[t] = psi_ref[:, 128 * t:128 * (t + 1)].astype(F32)
    ag_psi[p, 0] = cf[:, 0, :].astype(BF16)
    ag_psi[p, 1] = cf[:, 1, :].astype(BF16)
    ag_idx[p] = idx_ref[...]
    gb[b] = cf[b]
    nt = lambda u, w, **k: lax.dot_general(u, w, (((1,), (1,)), ((), ())), preferred_element_type=F32, **k)
    rows = psi_ref[...]
    pr, pi = nt(rows, beta_ref[0]), nt(rows, beta_ref[1])
    pj_send[...] = jnp.zeros_like(pj_send)
    pj_send[0:1, 0:72] = pr[0:1] + pi[1:2]
    pj_send[1:2, 0:72] = pr[1:2] - pi[0:1]
    pj_recv[p] = pj_send[...]
    m_ref[...] = jnp.zeros_like(m_ref)
    pl.semaphore_wait(barrier, N_PW + N_BAND - 2)

    agp = lambda peer, slot: copy_pw(ag_psi.at[p], ag_psi, agp_s, agp_r, peer, slot)
    agi = lambda peer, slot: copy_pw(ag_idx.at[p], ag_idx, agi_s, agi_r, peer, slot)
    pjc = lambda peer, slot: copy_pw(pj_send, pj_recv, pj_s, pj_r, peer, slot)
    gbc = lambda peer, slot: copy_band(cf.at[peer], gb, gb_s, gb_r, peer, slot)
    rbc = lambda peer, slot: copy_band(m_ref.at[peer], rb, rb_s, rb_r, peer, slot)
    qbc = lambda peer, slot: copy_band(q_send, qb, q_s, q_r, peer, slot)
    grc = lambda peer, slot: copy_pw(gs, gr, gr_s, gr_r, peer, slot)
    lrc = lambda peer, slot: copy_pw(ls.at[peer], lr, ls_s, lr_r, peer, slot)

    def start_first(s):
        q = pw_peer(p, s)
        agp(q, p).start()
        agi(q, p).start()
        pjc(q, p).start()
    each(1, N_PW, start_first)
    each(1, N_BAND, lambda s: gbc(band_peer(s), b).start())

    def forward(s):
        blk = pw_peer(p, s)

        @pl.when(s > 0)
        def _():
            agp(blk, blk).wait_recv()
            agi(blk, blk).wait_recv()
        forward_block(ag_psi[blk], ag_idx[blk], p, blk, f_ref, v_ref, li_ref, acc_ref, CH)
    each(0, N_PW, forward)

    each(1, N_PW, lambda s: pjc(pw_peer(p, s), pw_peer(p, s)).wait_recv())
    proj = pj_recv[0]
    for k in range(1, N_PW):
        proj = proj + pj_recv[k]
    pr_ref[...] = proj
    dc = jnp.dot(proj, bd_ref[0], precision=lax.Precision.HIGHEST, preferred_element_type=F32)
    qc = jnp.dot(proj, bd_ref[1], precision=lax.Precision.HIGHEST, preferred_element_type=F32)
    q_send[...] = qc[0:2].astype(BF16).astype(F32)
    qb[b] = q_send[...]
    pad = jnp.zeros((4, 128), F32)
    left = jnp.concatenate([dc[0:2], qc[0:2], pad], axis=0).astype(BF16)[:, :72]
    right = jnp.concatenate([-dc[1:2], dc[0:1], -qc[1:2], qc[0:1], pad], axis=0).astype(BF16)[:, :72]
    nl_ref[...] = (jnp.dot(left, beta_ref[0], preferred_element_type=F32)
                   + jnp.dot(right, beta_ref[1], preferred_element_type=F32))
    s_out[...] = (psi_ref[...].astype(F32) + nl_ref[2:4, :]).astype(BF16)

    each(1, N_BAND, lambda s: gbc(band_peer(s), band_peer(s)).wait_recv())
    gre, gim = gb[:, 0, :].astype(BF16), gb[:, 1, :].astype(BF16)
    m_ref[:, 0, 0:48] = nt(gre, gre) + nt(gim, gim)
    m_ref[:, 1, 0:48] = nt(gre, gim) - nt(gim, gre)
    rb[b] = m_ref[b]

    each(0, KD, lambda j: dense_plane(j, f_ref, vloc_ref, zp, zm, xp, xm))

    def start_rows(s):
        rbc(band_peer(s), b).start()
        qbc(band_peer(s), b).start()
    each(1, N_BAND, start_rows)

    def backward(i):
        blk = pw_peer(p, 15 - i)

        @pl.when(i == 13)
        def _():
            each(1, N_BAND, lambda s: rbc(band_peer(s), band_peer(s)).wait_recv())
            tot = rb[0]
            for k in range(1, N_BAND):
                tot = tot + rb[k]
            gs[...] = tot
            gr[p] = tot
        re, im = backward_block(ag_idx[blk], p, blk, f_ref, e_ref, li_ref, b_ref, s_ref, CHB)
        loc_ref[0] = re
        loc_ref[1] = im
        ls[blk, 0] = re.astype(BF16)
        ls[blk, 1] = im.astype(BF16)

        @pl.when(i > 0)
        def _():
            prev = pw_peer(p, 16 - i)
            lrc(prev, p).start()

        @pl.when(i == 14)
        def _():
            each(1, N_PW, lambda s: grc(pw_peer(p, s), p).start())
    each(0, N_PW, backward)

    x, y, z = split_index(idx_ref[...])
    x = x + (p * KD).astype(F32)
    fold = lambda v: jnp.where(v < 96.0, v, v - 192.0)
    kin = 4.0 * (fold(x) * fold(x) + fold(y) * fold(y) + fold(z) * fold(z)) * (1.0 / (NG * NG))
    loc_ref[0] += kin * cf[:, 0, :]
    loc_ref[1] += kin * cf[:, 1, :]

    each(1, N_BAND, lambda s: qbc(band_peer(s), band_peer(s)).wait_recv())
    proj = pr_ref[...]
    hp = lax.Precision.HIGHEST
    u, w = nt(proj, qb[:, 0, :], precision=hp), nt(proj, qb[:, 1, :], precision=hp)
    corr = jnp.concatenate([u[0:1] + w[1:2], w[0:1] - u[1:2]], axis=0)
    each(1, N_PW, lambda s: grc(pw_peer(p, s), pw_peer(p, s)).wait_recv())
    tot = gr[0]
    for k in range(1, N_PW):
        tot = tot + gr[k]
    g_out[...] = (tot[:, 0:48] + corr) * (1.0 / 98304.0)

    def add_part(s):
        src = pw_peer(p, 16 - s)
        lrc(src, src).wait_recv()
        loc_ref[...] += lr[src].astype(F32)
    each(1, N_PW, add_part)
    for t in range(48):
        sl = slice(128 * t, 128 * (t + 1))
        h = jnp.concatenate([loc_ref[0, t:t + 1, :], loc_ref[1, t:t + 1, :]], axis=0)
        h_ref[:, sl] = (h + nl_ref[0:2, sl]).astype(BF16)

    def drain_pw(s):
        q = pw_peer(p, s)
        for c in (agp, agi, pjc, grc, lrc):
            c(q, p).wait_send()
    each(1, N_PW, drain_pw)

    def drain_band(s):
        q = band_peer(s)
        for c in (gbc, rbc, qbc):
            c(q, b).wait_send()
    each(1, N_BAND, drain_band)


def on_device(psi, gvec_index, vloc, beta, dmat, qmat):
    rows = psi.reshape(2, 6144)
    idx = gvec_index.reshape(48, 128)
    planes = jnp.transpose(vloc, (1, 0, 2))
    mats = jnp.swapaxes(jnp.stack([dmat, qmat]), 2, 3)
    bd = sum(jnp.pad(mats[:, a], ((0, 0), (18 * a, 110 - 18 * a), (18 * a, 110 - 18 * a))) for a in range(4))
    tabs = [jnp.asarray(t) for t in dft_tables()]
    vm = pltpu.VMEM
    dma = pltpu.SemaphoreType.DMA
    full = pl.BlockSpec(memory_space=vm)
    h, s, g = pl.pallas_call(
        kernel,
        out_shape=(jax.ShapeDtypeStruct((2, 6144), BF16), jax.ShapeDtypeStruct((2, 6144), BF16),
                   jax.ShapeDtypeStruct((2, 48), F32)),
        in_specs=[full] * 9,
        out_specs=(full,) * 3,
        scratch_shapes=[
            vm((16, 24, 16, 256), F32), vm((48, 24, 128), F32), vm((48, 8, 128), F32), vm((216, 256), F32),
            vm((48, 48, 128), F32), vm((216, 256), F32), vm((2, 48, 8, 128), F32), vm((8, 6144), F32),
            vm((2, 48, 128), F32), vm((8, 128), F32),
            vm((16, 2, 48, 128), BF16), vm((16, 48, 128), jnp.int32), vm((8, 128), F32), vm((16, 8, 128), F32),
            vm((48, 2, 128), F32), vm((48, 2, 128), F32), vm((48, 2, 128), F32), vm((48, 2, 128), F32),
            vm((2, 128), F32), vm((48, 2, 128), F32), vm((2, 128), F32), vm((16, 2, 128), F32),
            vm((16, 2, 48, 128), BF16), vm((16, 2, 48, 128), BF16),
        ] + [dma((16,))] * 6 + [dma((48,))] * 6 + [dma((16,))] * 4,
        compiler_params=pltpu.CompilerParams(collective_id=0, has_side_effects=True,
                                             vmem_limit_bytes=48 * 1024 * 1024),
    )(rows, idx, planes, beta, bd, *tabs)
    return h[:, None, :], s[:, None, :], g[:, None, :]


def solution(mesh):
    in_specs = (P(None, "band", "pw"), P("pw"), P(None, "pw", None), P(None, None, "pw"), P(), P())
    out_specs = (P(None, "band", "pw"), P(None, "band", "pw"), P(None, "band", None))
    return jax.shard_map(
        on_device, mesh=mesh, in_specs=in_specs, out_specs=out_specs, check_vma=False
    )
```

profile of v0, /device:TPU:1, one launch (start us, length us, event | category | flops | bytes accessed | tf_op | source)
XLA Modules:
  0.0 135.2 jit_solution(12550444511060714201)
XLA Ops:
  0.6 0.9 copy.13
  1.5 0.9 copy.14
  2.4 0.1 pad_add_fusion.bd_ref
  2.5 0.0 copy-start
  2.5 1.7 %copy-done = f32[192,12,192]{2,0,1:T(8,128)S(1)} copy-done((f32[192,12,192]{2,0,1:T(8,128)S(1)}, f32[192,12,192]{2,0,1:T(8,128)}, u32[]{:S(2)}) %copy-start) | copy-done | bytes 1769496
  4.2 0.0 copy-start.1
  4.2 1.5 %copy-done.1 = bf16[2,72,6144]{2,1,0:T(8,128)(2,1)S(1)} copy-done((bf16[2,72,6144]{2,1,0:T(8,128)(2,1)S(1)}, bf16[2,72,6144]{2,1,0:T(8,128)(2,1)}, u32[]{:S(2)}) %copy-start.1) | copy-done | bytes 1769496
  5.7 0.0 copy-start.2
  5.7 1.0 copy-done.2
  6.7 0.0 copy-start.3
  6.7 1.0 copy-done.3
  7.7 0.0 copy-start.4
  7.7 1.0 copy-done.4
  8.7 0.0 copy-start.5
  8.7 1.0 copy-done.5
  9.7 0.0 copy-start.6
  9.7 0.7 copy-done.6
  10.5 0.0 copy-start.7
  10.5 0.7 copy-done.7
  11.2 122.2 %shard_map.121 = (bf16[2,6144]{1,0:T(2,128)(2,1)S(1)}, bf16[2,6144]{1,0:T(2,128)(2,1)S(1)}, f32[2,48]{1,0:T(2,128)S(1)}) custom-call(bf16[2,6144]{1,0:T(2,128)(2,1)S(1)} %bitcast.21, s32[48,128]{1,0:T(8,128)S(1)} %bitcast.22, f32[12,192,192]{2,1,0:T(8,128)S(1)} %bitcast.20, bf16[2,72,6144]{2,1,0:T(8,128)(2,1)S(1)} %copy-done.1, ...), custom_call_target="tpu_custom_call" | custom-call | tf_op jit(solution)/shard_map/pallas_call | solution.py:381
  133.4 0.6 copy.19
  134.0 0.6 copy.20
  134.7 0.6 copy.21
  (2 shorter events, 0.0 us)
Async XLA Ops:
  2.5 1.7 %copy-start = (f32[192,12,192]{2,0,1:T(8,128)S(1)}, f32[192,12,192]{2,0,1:T(8,128)}, u32[]{:S(2)}) copy-start(f32[192,12,192]{2,0,1:T(8,128)} %param.12) | copy-start | bytes 5308420
  4.2 1.5 %copy-start.1 = (bf16[2,72,6144]{2,1,0:T(8,128)(2,1)S(1)}, bf16[2,72,6144]{2,1,0:T(8,128)(2,1)}, u32[]{:S(2)}) copy-start(bf16[2,72,6144]{2,1,0:T(8,128)(2,1)} %beta_ref.1) | copy-start | bytes 5308420
  5.7 1.0 copy-start.2
  6.7 1.0 copy-start.3
  7.7 1.0 copy-start.4
  8.7 1.0 copy-start.5
  9.7 0.7 copy-start.6
  10.5 0.7 copy-start.7
where the time goes:
time: 136 us; the launch traced here: 135 us
  Pallas kernels  122 us (90%)
  local copies, waits for them, and re-layouts  12.2 us (9%)
    pallas_call x1, Pallas kernels, on_device(): pl.pallas_call(kernel, out_shape=(jax.ShapeDtypeStruct((2, 6144), BF16),...  122 us
    unnamed x21, local copies, waits for them, and re-layouts  12.2 us

commit v1 on v0

--- a/solution.py
+++ b/solution.py
@@ -9,8 +9,8 @@
 KD = 12
 F32, BF16 = jnp.float32, jnp.bfloat16
 TWO_PI = 2.0 * np.pi
-CH = 24
-CHB = 16
+CH = 48
+CHB = 48
 
 
 def dft_tables():
@@ -59,9 +59,10 @@
     m = mod_floor(y * p.astype(F32), 16.0)
     ar, ai = turn(jnp.where(m > 8.0, m - 16.0, m) * (1.0 / 16.0))
     wr, wi = turn(jnp.where(y > 96.0, y - 192.0, y) * np.float32(1.0 / NG))
+    ar, ai = ar * fac, ai * fac
     out = []
     for j in range(KD):
-        out.append(((ar * fac).astype(BF16).astype(F32), (ai * fac).astype(BF16).astype(F32)))
+        out.append((ar, ai))
         if j < KD - 1:
             ar, ai = ar * wr - ai * wi, ar * wi + ai * wr
     return out
@@ -71,8 +72,8 @@
     x, y, z = split_index(idx)
     w = x * NG + z
     hi = jnp.floor((w + 0.5) * (1.0 / 256.0))
-    li_ref[:, 0, :] = w - hi * 256.0
-    li_ref[:, 1, :] = hi
+    li_ref[0:48, :] = w - hi * 256.0
+    li_ref[48:96, :] = hi
     return phases(y, p)
 
 
@@ -80,7 +81,7 @@
     rows = lax.broadcasted_iota(jnp.int32, (256, 128), 0).astype(F32).astype(BF16)
     parts = []
     for k in range(n):
-        lo = li_ref[t + k, 0:1, :].astype(BF16)
+        lo = li_ref[t + k:t + k + 1, :].astype(BF16)
         parts.append(jnp.where(rows == lo, jnp.array(1, BF16), jnp.array(0, BF16)))
     return jnp.concatenate(parts, axis=1) if n > 1 else parts[0]
 
@@ -89,9 +90,9 @@
     upper = (lax.broadcasted_iota(jnp.int32, (48, 128), 0) >= 24).astype(F32)
     cols = []
     for k in range(n):
-        v = v_ref[t + k]
+        v = v_ref[24 * (t + k):24 * (t + k) + 24, :]
         v = jnp.concatenate([v, v], axis=0).astype(BF16)
-        h = (li_ref[t + k, 1:2, :] - upper).astype(BF16)
+        h = (li_ref[48 + t + k:49 + t + k, :] - upper).astype(BF16)
         zero = jnp.zeros_like(v)
         rows = [jnp.where(h == jnp.array(2 * q, BF16), v, zero) for q in range(4)]
         rows.append(jnp.where(h == jnp.array(8, BF16), v, zero)[:24])
@@ -104,8 +105,8 @@
     pr, pi = psi[0].astype(F32), psi[1].astype(F32)
     for j in range(KD):
         er, ei = e[j]
-        v_ref[:, j, :] = pr * er - pi * ei
-        v_ref[:, KD + j, :] = pr * ei + pi * er
+        v_ref[pl.ds(j, 48, stride=24), :] = pr * er - pi * ei
+        v_ref[pl.ds(KD + j, 48, stride=24), :] = pr * ei + pi * er
     acc_ref[...] = jnp.zeros_like(acc_ref)
 
     def step(i, carry):
@@ -114,7 +115,10 @@
         l = spread(v_ref, li_ref, t, ch)
         acc_ref[...] += lax.dot_general(l, zt, (((1,), (1,)), ((), ())), preferred_element_type=F32)
         return carry
-    lax.fori_loop(0, 48 // ch, step, 0)
+    if ch == 48:
+        step(0, 0)
+    else:
+        lax.fori_loop(0, 48 // ch, step, 0)
     left = lax.broadcasted_iota(jnp.int32, (24, 128), 1) < 64
     for g in range(3):
         a = [[acc_ref[(3 * g + h) * 24:(3 * g + h + 1) * 24, 128 * q:128 * (q + 1)] for q in range(2)] for h in range(3)]
@@ -122,38 +126,44 @@
         r20, r21 = pltpu.roll(a[2][0], 64, 1), pltpu.roll(a[2][1], 64, 1)
         pieces = [(a[0][0], a[0][1]), (jnp.where(left, r01, r10), r10), (a[1][1], a[2][0]), (jnp.where(left, r20, r21), r21)]
         for k, (low, high) in enumerate(pieces):
-            f_ref[base, :, 4 * g + k, 0:128] = low
-            f_ref[base, :, 4 * g + k, 128:256] = high
-    f_ref[base, :, KD:16, :] = jnp.zeros((24, 16 - KD, 256), F32)
+            rows = pl.ds(base * 16 + 4 * g + k, 24, stride=256)
+            f_ref[0, rows, :] = low
+            f_ref[1, rows, :] = high
+    for k in range(KD, 16):
+        rows = pl.ds(base * 16 + k, 24, stride=256)
+        f_ref[0, rows, :] = jnp.zeros((24, 128), F32)
+        f_ref[1, rows, :] = jnp.zeros((24, 128), F32)
 
 
 def dense_plane(j, f_ref, vloc_ref, zp, zm, xp, xm):
     dot = lambda a, b: jnp.dot(a, b, preferred_element_type=F32)
-    fr, fi = (f_ref[:, c * KD + j].reshape(256, 256).astype(BF16) for c in range(2))
-    y = dot(jnp.concatenate([fr, fi], axis=1), zp[...]).astype(BF16)
+    rows = [pl.ds(pl.multiple_of((c * KD + j) * 256, 256), 256) for c in range(2)]
+    y = jnp.concatenate([f_ref[q, rows[c], :].astype(BF16) for c in range(2) for q in range(2)], axis=1)
+    y = dot(y, zp[...]).astype(BF16)
     y = jnp.concatenate([y[:, 0:NG], y[:, 256:256 + NG]], axis=0)
     s = dot(xp[...], y)
     v = vloc_ref[j]
     s = jnp.concatenate([s[:NG] * v, s[NG:] * v], axis=0).astype(BF16)
     s = dot(xm[...], s).astype(BF16)
     out = dot(s[:256], zm[0:NG, :]) + dot(s[256:], zm[256:256 + NG, :])
-    f_ref[:, j] = out[:, :256].reshape(16, 16, 256)
-    f_ref[:, KD + j] = out[:, 256:].reshape(16, 16, 256)
-
-
-def backward_block(idx, p, base, f_ref, e_ref, li_ref, b_ref, s_ref, ch):
+    for c in range(2):
+        for q in range(2):
+            f_ref[q, rows[c], :] = out[:, 128 * (2 * c + q):128 * (2 * c + q + 1)]
+
+
+def backward_block(idx, p, base, f_ref, e_ref, li_ref, b_ref, s_ref, ch, middle=lambda: None):
     e = prep_index(idx, p, li_ref)
     for j in range(KD):
         er, ei = e[j]
-        e_ref[:, j, :] = er
-        e_ref[:, KD + j, :] = ei
-        e_ref[:, 2 * KD + j, :] = -ei
-        e_ref[:, 3 * KD + j, :] = er
+        e_ref[pl.ds(j, 48, stride=48), :] = er
+        e_ref[pl.ds(KD + j, 48, stride=48), :] = ei
+        e_ref[pl.ds(2 * KD + j, 48, stride=48), :] = -ei
+        e_ref[pl.ds(3 * KD + j, 48, stride=48), :] = er
     left = lax.broadcasted_iota(jnp.int32, (24, 128), 1) < 64
     for g in range(3):
         x = []
         for k in range(4):
-            x.append([f_ref[base, :, 4 * g + k, 128 * q:128 * (q + 1)] for q in range(2)])
+            x.append([f_ref[q, pl.ds(base * 16 + 4 * g + k, 24, stride=256), :] for q in range(2)])
         r10, r11 = pltpu.roll(x[1][0], 64, 1), pltpu.roll(x[1][1], 64, 1)
         r30, r31 = pltpu.roll(x[3][0], 64, 1), pltpu.roll(x[3][1], 64, 1)
         pieces = [(x[0][0], jnp.where(left, x[0][1], r10)), (jnp.where(left, r10, r11), x[2][0]),
@@ -163,26 +173,30 @@
             b_ref[r:r + 24, 0:128] = low
             b_ref[r:r + 24, 128:256] = high
 
+    middle()
     bm = b_ref[...].astype(BF16)
 
     def step(i, carry):
         t = i * ch
         tt = jnp.dot(bm, one_hot(li_ref, t, ch), preferred_element_type=F32)
         for k in range(ch):
-            hi = jnp.broadcast_to(li_ref[t + k, 1:2, :], (24, 128))
+            hi = jnp.broadcast_to(li_ref[48 + t + k:49 + t + k, :], (24, 128))
             sel = tt[0:24, 128 * k:128 * (k + 1)]
             for h in range(1, 9):
                 sel = jnp.where(hi == float(h), tt[24 * h:24 * (h + 1), 128 * k:128 * (k + 1)], sel)
-            ev = e_ref[t + k]
+            ev = e_ref[48 * (t + k):48 * (t + k) + 48, :]
             a, b = sel * ev[:24], sel * ev[24:]
-            s_ref[0, t + k] = a[0:8] + a[8:16] + a[16:24]
-            s_ref[1, t + k] = b[0:8] + b[8:16] + b[16:24]
+            s_ref[8 * (t + k):8 * (t + k) + 8, :] = a[0:8] + a[8:16] + a[16:24]
+            s_ref[384 + 8 * (t + k):392 + 8 * (t + k), :] = b[0:8] + b[8:16] + b[16:24]
         return carry
-    lax.fori_loop(0, 48 // ch, step, 0)
-    re, im = s_ref[0, :, 0, :], s_ref[1, :, 0, :]
+    if ch == 48:
+        step(0, 0)
+    else:
+        lax.fori_loop(0, 48 // ch, step, 0)
+    re, im = (s_ref[pl.ds(c, 48, stride=8), :] for c in (0, 384))
     for k in range(1, 8):
-        re = re + s_ref[0, :, k, :]
-        im = im + s_ref[1, :, k, :]
+        re = re + s_ref[pl.ds(k, 48, stride=8), :]
+        im = im + s_ref[pl.ds(384 + k, 48, stride=8), :]
     return re, im
 
 
@@ -197,7 +211,8 @@
     return 2 * y + lax.rem(p + s, 2)
 
 
-def kernel(psi_ref, idx_ref, vloc_ref, beta_ref, bd_ref, zp, zm, xp, xm, h_ref, s_out, g_out,
+def kernel(psi_hbm, idx_hbm, vloc_hbm, beta_hbm, d_hbm, q_hbm, zp_hbm, zm_hbm, xp_hbm, xm_hbm, h_ref, s_out, g_out,
+           psi_ref, idx_ref, vloc_ref, beta_ref, d_ref, q_ref, zp, zm, xp, xm, bd_ref, corr_ref, in_sem,
            f_ref, v_ref, li_ref, acc_ref, e_ref, b_ref, s_ref, nl_ref, loc_ref, pr_ref,
            ag_psi, ag_idx, pj_send, pj_recv, cf, gb, m_ref, rb, q_send, qb, gs, gr, ls, lr,
            agp_s, agp_r, agi_s, agi_r, pj_s, pj_r, gb_s, gb_r, rb_s, rb_r, q_s, q_r, gr_s, gr_r, ls_s, lr_r):
@@ -222,12 +237,19 @@
             return carry
         lax.fori_loop(first, last, step, 0)
 
+    loads = [pltpu.make_async_copy(src, dst, in_sem.at[k]) for k, (src, dst) in enumerate((
+        (psi_hbm, psi_ref), (idx_hbm, idx_ref), (beta_hbm, beta_ref), (d_hbm, d_ref), (q_hbm, q_ref),
+        (vloc_hbm, vloc_ref), (zp_hbm, zp), (zm_hbm, zm), (xp_hbm, xp), (xm_hbm, xm)))]
+    for load in loads:
+        load.start()
     barrier = pltpu.get_barrier_semaphore()
     each(1, N_PW, lambda s: pl.semaphore_signal(barrier, inc=1, device_id={"pw": pw_peer(p, s)},
                                                 device_id_type=pl.DeviceIdType.MESH))
     each(1, N_BAND, lambda s: pl.semaphore_signal(barrier, inc=1, device_id={"band": band_peer(s)},
                                                   device_id_type=pl.DeviceIdType.MESH))
 
+    loads[0].wait()
+    loads[1].wait()
     for t in range(48):
         cf[t] = psi_ref[:, 128 * t:128 * (t + 1)].astype(F32)
     ag_psi[p, 0] = cf[:, 0, :].astype(BF16)
@@ -235,15 +257,6 @@
     ag_idx[p] = idx_ref[...]
     gb[b] = cf[b]
     nt = lambda u, w, **k: lax.dot_general(u, w, (((1,), (1,)), ((), ())), preferred_element_type=F32, **k)
-    rows = psi_ref[...]
-    pr, pi = nt(rows, beta_ref[0]), nt(rows, beta_ref[1])
-    pj_send[...] = jnp.zeros_like(pj_send)
-    pj_send[0:1, 0:72] = pr[0:1] + pi[1:2]
-    pj_send[1:2, 0:72] = pr[1:2] - pi[0:1]
-    pj_recv[p] = pj_send[...]
-    m_ref[...] = jnp.zeros_like(m_ref)
-    pl.semaphore_wait(barrier, N_PW + N_BAND - 2)
-
     agp = lambda peer, slot: copy_pw(ag_psi.at[p], ag_psi, agp_s, agp_r, peer, slot)
     agi = lambda peer, slot: copy_pw(ag_idx.at[p], ag_idx, agi_s, agi_r, peer, slot)
     pjc = lambda peer, slot: copy_pw(pj_send, pj_recv, pj_s, pj_r, peer, slot)
@@ -253,22 +266,52 @@
     grc = lambda peer, slot: copy_pw(gs, gr, gr_s, gr_r, peer, slot)
     lrc = lambda peer, slot: copy_pw(ls.at[peer], lr, ls_s, lr_r, peer, slot)
 
+    loads[2].wait()
+    rows = psi_ref[...]
+    pr, pi = nt(rows, beta_ref[0]), nt(rows, beta_ref[1])
+    pj_send[...] = jnp.zeros_like(pj_send)
+    pj_send[0:1, 0:72] = pr[0:1] + pi[1:2]
+    pj_send[1:2, 0:72] = pr[1:2] - pi[0:1]
+    pj_recv[p] = pj_send[...]
+    m_ref[...] = jnp.zeros_like(m_ref)
+    partner = pw_peer(p, 1)
+
     def start_first(s):
         q = pw_peer(p, s)
-        agp(q, p).start()
-        agi(q, p).start()
         pjc(q, p).start()
-    each(1, N_PW, start_first)
-    each(1, N_BAND, lambda s: gbc(band_peer(s), b).start())
+
+        @pl.when(jnp.logical_or(s == 1, lax.rem(s, 2) == 0))
+        def _():
+            agp(q, p).start()
+            agi(q, p).start()
+
+    def pass_on(blk):
+        slot = 2 * lax.div(blk, 2) + 1 - lax.rem(blk, 2)
+        return [pltpu.make_async_remote_copy(src_ref=buf.at[blk], dst_ref=buf.at[blk], send_sem=ssem.at[slot],
+                                             recv_sem=rsem.at[blk], device_id={"pw": partner},
+                                             device_id_type=pl.DeviceIdType.MESH)
+                for buf, ssem, rsem in ((ag_psi, agp_s, agp_r), (ag_idx, agi_s, agi_r))]
 
     def forward(s):
         blk = pw_peer(p, s)
-
-        @pl.when(s > 0)
-        def _():
-            agp(blk, blk).wait_recv()
-            agi(blk, blk).wait_recv()
         forward_block(ag_psi[blk], ag_idx[blk], p, blk, f_ref, v_ref, li_ref, acc_ref, CH)
+
+        @pl.when(s == 0)
+        def _():
+            pl.semaphore_wait(barrier, N_PW + N_BAND - 2)
+            each(1, N_PW, start_first)
+            each(1, N_BAND, lambda s: gbc(band_peer(s), b).start())
+
+        @pl.when(s < N_PW - 1)
+        def _():
+            new = pw_peer(p, s + 1)
+            agp(new, new).wait_recv()
+            agi(new, new).wait_recv()
+
+        @pl.when(jnp.logical_and(s < N_PW - 1, lax.rem(s, 2) == 1))
+        def _():
+            for copy in pass_on(pw_peer(p, s + 1)):
+                copy.start()
     each(0, N_PW, forward)
 
     each(1, N_PW, lambda s: pjc(pw_peer(p, s), pw_peer(p, s)).wait_recv())
@@ -276,8 +319,15 @@
     for k in range(1, N_PW):
         proj = proj + pj_recv[k]
     pr_ref[...] = proj
-    dc = jnp.dot(proj, bd_ref[0], precision=lax.Precision.HIGHEST, preferred_element_type=F32)
-    qc = jnp.dot(proj, bd_ref[1], precision=lax.Precision.HIGHEST, preferred_element_type=F32)
+    for k in range(3, 10):
+        loads[k].wait()
+    bd_ref[...] = jnp.zeros_like(bd_ref)
+    for a in range(4):
+        sl = slice(18 * a, 18 * a + 18)
+        bd_ref[0, sl, sl] = d_ref[:, a, :]
+        bd_ref[1, sl, sl] = q_ref[:, a, :]
+    dc = nt(proj, bd_ref[0], precision=lax.Precision.HIGHEST)
+    qc = nt(proj, bd_ref[1], precision=lax.Precision.HIGHEST)
     q_send[...] = qc[0:2].astype(BF16).astype(F32)
     qb[b] = q_send[...]
     pad = jnp.zeros((4, 128), F32)
@@ -293,7 +343,10 @@
     m_ref[:, 1, 0:48] = nt(gre, gim) - nt(gim, gre)
     rb[b] = m_ref[b]
 
-    each(0, KD, lambda j: dense_plane(j, f_ref, vloc_ref, zp, zm, xp, xm))
+    def dense(j):
+        dense_plane(2 * j, f_ref, vloc_ref, zp, zm, xp, xm)
+        dense_plane(2 * j + 1, f_ref, vloc_ref, zp, zm, xp, xm)
+    each(0, KD // 2, dense)
 
     def start_rows(s):
         rbc(band_peer(s), b).start()
@@ -303,26 +356,31 @@
     def backward(i):
         blk = pw_peer(p, 15 - i)
 
-        @pl.when(i == 13)
+        def middle():
+            @pl.when(i > 0)
+            def _():
+                lrc(pw_peer(p, 16 - i), p).start()
+        re, im = backward_block(ag_idx[blk], p, blk, f_ref, e_ref, li_ref, b_ref, s_ref, CHB, middle)
+        loc_ref[0] = re
+        loc_ref[1] = im
+        ls[blk, 0] = re.astype(BF16)
+        ls[blk, 1] = im.astype(BF16)
+
+        @pl.when(i == 7)
         def _():
             each(1, N_BAND, lambda s: rbc(band_peer(s), band_peer(s)).wait_recv())
+            each(1, N_BAND, lambda s: qbc(band_peer(s), band_peer(s)).wait_recv())
             tot = rb[0]
             for k in range(1, N_BAND):
                 tot = tot + rb[k]
             gs[...] = tot
             gr[p] = tot
-        re, im = backward_block(ag_idx[blk], p, blk, f_ref, e_ref, li_ref, b_ref, s_ref, CHB)
-        loc_ref[0] = re
-        loc_ref[1] = im
-        ls[blk, 0] = re.astype(BF16)
-        ls[blk, 1] = im.astype(BF16)
-
-        @pl.when(i > 0)
-        def _():
-            prev = pw_peer(p, 16 - i)
-            lrc(prev, p).start()
-
-        @pl.when(i == 14)
+            proj = pr_ref[...]
+            hp = lax.Precision.HIGHEST
+            u, w = nt(proj, qb[:, 0, :], precision=hp), nt(proj, qb[:, 1, :], precision=hp)
+            corr_ref[...] = jnp.concatenate([u[0:1] + w[1:2], w[0:1] - u[1:2]], axis=0)
+
+        @pl.when(i == 8)
         def _():
             each(1, N_PW, lambda s: grc(pw_peer(p, s), p).start())
     each(0, N_PW, backward)
@@ -334,16 +392,11 @@
     loc_ref[0] += kin * cf[:, 0, :]
     loc_ref[1] += kin * cf[:, 1, :]
 
-    each(1, N_BAND, lambda s: qbc(band_peer(s), band_peer(s)).wait_recv())
-    proj = pr_ref[...]
-    hp = lax.Precision.HIGHEST
-    u, w = nt(proj, qb[:, 0, :], precision=hp), nt(proj, qb[:, 1, :], precision=hp)
-    corr = jnp.concatenate([u[0:1] + w[1:2], w[0:1] - u[1:2]], axis=0)
     each(1, N_PW, lambda s: grc(pw_peer(p, s), pw_peer(p, s)).wait_recv())
     tot = gr[0]
     for k in range(1, N_PW):
         tot = tot + gr[k]
-    g_out[...] = (tot[:, 0:48] + corr) * (1.0 / 98304.0)
+    g_out[...] = (tot[:, 0:48] + corr_ref[...]) * (1.0 / 98304.0)
 
     def add_part(s):
         src = pw_peer(p, 16 - s)
@@ -372,8 +425,7 @@
     rows = psi.reshape(2, 6144)
     idx = gvec_index.reshape(48, 128)
     planes = jnp.transpose(vloc, (1, 0, 2))
-    mats = jnp.swapaxes(jnp.stack([dmat, qmat]), 2, 3)
-    bd = sum(jnp.pad(mats[:, a], ((0, 0), (18 * a, 110 - 18 * a), (18 * a, 110 - 18 * a))) for a in range(4))
+    mats = [jnp.transpose(m, (1, 0, 2)) for m in (dmat, qmat)]
     tabs = [jnp.asarray(t) for t in dft_tables()]
     vm = pltpu.VMEM
     dma = pltpu.SemaphoreType.DMA
@@ -382,11 +434,14 @@
         kernel,
         out_shape=(jax.ShapeDtypeStruct((2, 6144), BF16), jax.ShapeDtypeStruct((2, 6144), BF16),
                    jax.ShapeDtypeStruct((2, 48), F32)),
-        in_specs=[full] * 9,
+        in_specs=[pl.BlockSpec(memory_space=pl.ANY)] * 10,
         out_specs=(full,) * 3,
         scratch_shapes=[
-            vm((16, 24, 16, 256), F32), vm((48, 24, 128), F32), vm((48, 8, 128), F32), vm((216, 256), F32),
-            vm((48, 48, 128), F32), vm((216, 256), F32), vm((2, 48, 8, 128), F32), vm((8, 6144), F32),
+            vm((2, 6144), BF16), vm((48, 128), jnp.int32), vm((KD, NG, NG), F32), vm((2, 72, 6144), BF16),
+            vm((18, 4, 18), F32), vm((18, 4, 18), F32), vm((512, 512), BF16), vm((512, 512), BF16),
+            vm((384, 512), BF16), vm((512, 384), BF16), vm((2, 128, 128), F32), vm((2, 48), F32), dma((10,)),
+            vm((2, 6400, 128), F32), vm((1176, 128), F32), vm((96, 128), F32), vm((216, 256), F32),
+            vm((2352, 128), F32), vm((216, 256), F32), vm((776, 128), F32), vm((8, 6144), F32),
             vm((2, 48, 128), F32), vm((8, 128), F32),
             vm((16, 2, 48, 128), BF16), vm((16, 48, 128), jnp.int32), vm((8, 128), F32), vm((16, 8, 128), F32),
             vm((48, 2, 128), F32), vm((48, 2, 128), F32), vm((48, 2, 128), F32), vm((48, 2, 128), F32),
@@ -394,8 +449,8 @@
             vm((16, 2, 48, 128), BF16), vm((16, 2, 48, 128), BF16),
         ] + [dma((16,))] * 6 + [dma((48,))] * 6 + [dma((16,))] * 4,
         compiler_params=pltpu.CompilerParams(collective_id=0, has_side_effects=True,
-                                             vmem_limit_bytes=48 * 1024 * 1024),
-    )(rows, idx, planes, beta, bd, *tabs)
+                                             vmem_limit_bytes=60 * 1024 * 1024),
+    )(rows, idx, planes, beta, *mats, *tabs)
     return h[:, None, :], s[:, None, :], g[:, None, :]
 
 

time: 136 us -> 101 us (0.74)
  Pallas kernels: 122 us -> 95.2 us
  local copies, waits for them, and re-layouts: 12.2 us -> 3.92 us
    pallas_call x1, Pallas kernels: 122 us -> 95.2 us  [on_device(): pl.pallas_call(kernel, out_shape=(jax.ShapeDtypeStruct((2, 6144), BF16),...]
    unnamed x21 -> x3, local copies, waits for them, and re-layouts: 12.2 us -> 3.92 us
where the time goes in v1:
time: 101 us; the launch traced here: 99.8 us
  Pallas kernels  95.2 us (94%)
  local copies, waits for them, and re-layouts  3.92 us (4%)
    pallas_call x1, Pallas kernels, on_device(): pl.pallas_call(kernel, out_shape=(jax.ShapeDtypeStruct((2, 6144), BF16),...  95.2 us
    unnamed x3, local copies, waits for them, and re-layouts  3.92 us

profile of v1, /device:TPU:1, one launch (start us, length us, event | category | flops | bytes accessed | tf_op | source)
XLA Modules:
  0.0 99.8 jit_solution(6030194078032578123)
XLA Ops:
  0.6 95.2 %shard_map.121 = (bf16[2,6144]{1,0:T(2,128)(2,1)}, bf16[2,6144]{1,0:T(2,128)(2,1)}, f32[2,48]{1,0:T(2,128)}) custom-call(bf16[2,6144]{1,0:T(2,128)(2,1)} %bitcast.13, s32[48,128]{1,0:T(8,128)} %bitcast.14, f32[12,192,192]{2,1,0:T(8,128)} %bitcast.10, bf16[2,72,6144]{2,1,0:T(8,128)(2,1)} %beta_hbm.1, f32[18,4,18]{2,1,0:T(4,128)} %bitcast.11, ...), custom_call_target="tpu_custom_call" | custom-call | tf_op jit(solution)/shard_map/pallas_call | solution.py:433
  95.9 1.4 %copy.17 = bf16[2,1,6144]{2,0,1:T(2,128)(2,1)} copy(bf16[2,1,6144]{2,0,1:T(2,128)(2,1)} %bitcast.16) | data formatting | bytes 49152
  97.2 1.4 %copy.18 = bf16[2,1,6144]{2,0,1:T(2,128)(2,1)} copy(bf16[2,1,6144]{2,0,1:T(2,128)(2,1)} %bitcast.15) | data formatting | bytes 49152
  98.6 1.2 %copy.19 = f32[2,1,48]{2,1,0:T(1,128)} copy(f32[2,1,48]{2,1,0:T(1,128)} %bitcast.17) | data formatting | bytes 768

commit v2 on v1

--- a/solution.py
+++ b/solution.py
@@ -214,22 +214,16 @@
 def kernel(psi_hbm, idx_hbm, vloc_hbm, beta_hbm, d_hbm, q_hbm, zp_hbm, zm_hbm, xp_hbm, xm_hbm, h_ref, s_out, g_out,
            psi_ref, idx_ref, vloc_ref, beta_ref, d_ref, q_ref, zp, zm, xp, xm, bd_ref, corr_ref, in_sem,
            f_ref, v_ref, li_ref, acc_ref, e_ref, b_ref, s_ref, nl_ref, loc_ref, pr_ref,
-           ag_psi, ag_idx, pj_send, pj_recv, cf, gb, m_ref, rb, q_send, qb, gs, gr, ls, lr,
-           agp_s, agp_r, agi_s, agi_r, pj_s, pj_r, gb_s, gb_r, rb_s, rb_r, q_s, q_r, gr_s, gr_r, ls_s, lr_r):
+           ag_psi, ag_idx, pj_send, pj_recv, cf, gb, m_ref, rb, gs, gr, ls, lr,
+           agp_r, agi_r, agp_s, agi_s, pj_s, pj_r, gb_s, gb_r, rb_s, rb_r, gr_s, gr_r, ls_s, lr_r):
     p, b = lax.axis_index("pw"), lax.axis_index("band")
 
     def band_peer(s):
         return lax.rem(b + s, N_BAND)
 
-    def copy_pw(src, dst, ssem, rsem, peer, slot):
-        return pltpu.make_async_remote_copy(src_ref=src, dst_ref=dst.at[slot], send_sem=ssem.at[peer],
-                                            recv_sem=rsem.at[slot], device_id={"pw": peer},
-                                            device_id_type=pl.DeviceIdType.MESH)
-
-    def copy_band(src, dst, ssem, rsem, peer, slot):
-        return pltpu.make_async_remote_copy(src_ref=src, dst_ref=dst.at[slot], send_sem=ssem.at[peer],
-                                            recv_sem=rsem.at[slot], device_id={"band": peer},
-                                            device_id_type=pl.DeviceIdType.MESH)
+    def copy(src, dst, ssem, rsem, **peer):
+        return pltpu.make_async_remote_copy(src_ref=src, dst_ref=dst, send_sem=ssem, recv_sem=rsem,
+                                            device_id=peer, device_id_type=pl.DeviceIdType.MESH)
 
     def each(first, last, body):
         def step(s, carry):
@@ -257,14 +251,17 @@
     ag_idx[p] = idx_ref[...]
     gb[b] = cf[b]
     nt = lambda u, w, **k: lax.dot_general(u, w, (((1,), (1,)), ((), ())), preferred_element_type=F32, **k)
-    agp = lambda peer, slot: copy_pw(ag_psi.at[p], ag_psi, agp_s, agp_r, peer, slot)
-    agi = lambda peer, slot: copy_pw(ag_idx.at[p], ag_idx, agi_s, agi_r, peer, slot)
-    pjc = lambda peer, slot: copy_pw(pj_send, pj_recv, pj_s, pj_r, peer, slot)
-    gbc = lambda peer, slot: copy_band(cf.at[peer], gb, gb_s, gb_r, peer, slot)
-    rbc = lambda peer, slot: copy_band(m_ref.at[peer], rb, rb_s, rb_r, peer, slot)
-    qbc = lambda peer, slot: copy_band(q_send, qb, q_s, q_r, peer, slot)
-    grc = lambda peer, slot: copy_pw(gs, gr, gr_s, gr_r, peer, slot)
-    lrc = lambda peer, slot: copy_pw(ls.at[peer], lr, ls_s, lr_r, peer, slot)
+    agp = lambda peer, slot: copy(ag_psi.at[p], ag_psi.at[slot], agp_s, agp_r.at[slot], pw=peer)
+    agi = lambda peer, slot: copy(ag_idx.at[p], ag_idx.at[slot], agi_s, agi_r.at[slot], pw=peer)
+    partner = pw_peer(p, 1)
+
+    def all_of(buf, n, ssem, rsem):
+        return copy(buf.at[pl.ds(0, n)], buf.at[pl.ds(0, n)], ssem, rsem, pw=partner)
+    pj_all = all_of(pj_recv, N_PW - 1, pj_s, pj_r)
+    gb_all = all_of(gb, N_BAND - 1, gb_s, gb_r)
+    rb_all = all_of(rb, N_BAND - 1, rb_s, rb_r)
+    gr_all = all_of(gr, N_PW - 1, gr_s, gr_r)
+    lr_all = all_of(lr, N_PW - 1, ls_s, lr_r)
 
     loads[2].wait()
     rows = psi_ref[...]
@@ -274,23 +271,22 @@
     pj_send[1:2, 0:72] = pr[1:2] - pi[0:1]
     pj_recv[p] = pj_send[...]
     m_ref[...] = jnp.zeros_like(m_ref)
-    partner = pw_peer(p, 1)
 
     def start_first(s):
         q = pw_peer(p, s)
-        pjc(q, p).start()
-
-        @pl.when(jnp.logical_or(s == 1, lax.rem(s, 2) == 0))
-        def _():
-            agp(q, p).start()
-            agi(q, p).start()
+        agp(q, p).start()
+        agi(q, p).start()
+
+    def start_proj(s):
+        copy(pj_send, pj_recv.at[p], pj_s, pj_r, pw=pw_peer(p, s)).start()
+
+    def start_chunk(s):
+        q = band_peer(s)
+        copy(cf.at[q], gb.at[b], gb_s, gb_r, band=q).start()
 
     def pass_on(blk):
-        slot = 2 * lax.div(blk, 2) + 1 - lax.rem(blk, 2)
-        return [pltpu.make_async_remote_copy(src_ref=buf.at[blk], dst_ref=buf.at[blk], send_sem=ssem.at[slot],
-                                             recv_sem=rsem.at[blk], device_id={"pw": partner},
-                                             device_id_type=pl.DeviceIdType.MESH)
-                for buf, ssem, rsem in ((ag_psi, agp_s, agp_r), (ag_idx, agi_s, agi_r))]
+        copy(ag_psi.at[blk], ag_psi.at[blk], agp_s, agp_r.at[blk], pw=partner).start()
+        copy(ag_idx.at[blk], ag_idx.at[blk], agi_s, agi_r.at[blk], pw=partner).start()
 
     def forward(s):
         blk = pw_peer(p, s)
@@ -299,8 +295,10 @@
         @pl.when(s == 0)
         def _():
             pl.semaphore_wait(barrier, N_PW + N_BAND - 2)
-            each(1, N_PW, start_first)
-            each(1, N_BAND, lambda s: gbc(band_peer(s), b).start())
+            start_first(1)
+            each(1, N_PW // 2, lambda k: start_first(2 * k))
+            each(1, N_PW, start_proj)
+            each(1, N_BAND, start_chunk)
 
         @pl.when(s < N_PW - 1)
         def _():
@@ -310,11 +308,10 @@
 
         @pl.when(jnp.logical_and(s < N_PW - 1, lax.rem(s, 2) == 1))
         def _():
-            for copy in pass_on(pw_peer(p, s + 1)):
-                copy.start()
+            pass_on(pw_peer(p, s + 1))
     each(0, N_PW, forward)
 
-    each(1, N_PW, lambda s: pjc(pw_peer(p, s), pw_peer(p, s)).wait_recv())
+    pj_all.wait_recv()
     proj = pj_recv[0]
     for k in range(1, N_PW):
         proj = proj + pj_recv[k]
@@ -328,16 +325,17 @@
         bd_ref[1, sl, sl] = q_ref[:, a, :]
     dc = nt(proj, bd_ref[0], precision=lax.Precision.HIGHEST)
     qc = nt(proj, bd_ref[1], precision=lax.Precision.HIGHEST)
-    q_send[...] = qc[0:2].astype(BF16).astype(F32)
-    qb[b] = q_send[...]
+    qc = qc.astype(BF16).astype(F32)
+    m_ref[:, 2, :] = jnp.broadcast_to(qc[0:1], (48, 128))
+    m_ref[:, 3, :] = jnp.broadcast_to(qc[1:2], (48, 128))
     pad = jnp.zeros((4, 128), F32)
     left = jnp.concatenate([dc[0:2], qc[0:2], pad], axis=0).astype(BF16)[:, :72]
     right = jnp.concatenate([-dc[1:2], dc[0:1], -qc[1:2], qc[0:1], pad], axis=0).astype(BF16)[:, :72]
     nl_ref[...] = (jnp.dot(left, beta_ref[0], preferred_element_type=F32)
                    + jnp.dot(right, beta_ref[1], preferred_element_type=F32))
-    s_out[...] = (psi_ref[...].astype(F32) + nl_ref[2:4, :]).astype(BF16)
-
-    each(1, N_BAND, lambda s: gbc(band_peer(s), band_peer(s)).wait_recv())
+    s_out[...] = psi_ref[...].astype(F32) + nl_ref[2:4, :]
+
+    gb_all.wait_recv()
     gre, gim = gb[:, 0, :].astype(BF16), gb[:, 1, :].astype(BF16)
     m_ref[:, 0, 0:48] = nt(gre, gre) + nt(gim, gim)
     m_ref[:, 1, 0:48] = nt(gre, gim) - nt(gim, gre)
@@ -349,8 +347,8 @@
     each(0, KD // 2, dense)
 
     def start_rows(s):
-        rbc(band_peer(s), b).start()
-        qbc(band_peer(s), b).start()
+        q = band_peer(s)
+        copy(m_ref.at[q], rb.at[b], rb_s, rb_r, band=q).start()
     each(1, N_BAND, start_rows)
 
     def backward(i):
@@ -359,7 +357,8 @@
         def middle():
             @pl.when(i > 0)
             def _():
-                lrc(pw_peer(p, 16 - i), p).start()
+                q = pw_peer(p, 16 - i)
+                copy(ls.at[q], lr.at[p], ls_s, lr_r, pw=q).start()
         re, im = backward_block(ag_idx[blk], p, blk, f_ref, e_ref, li_ref, b_ref, s_ref, CHB, middle)
         loc_ref[0] = re
         loc_ref[1] = im
@@ -368,21 +367,20 @@
 
         @pl.when(i == 7)
         def _():
-            each(1, N_BAND, lambda s: rbc(band_peer(s), band_peer(s)).wait_recv())
-            each(1, N_BAND, lambda s: qbc(band_peer(s), band_peer(s)).wait_recv())
+            rb_all.wait_recv()
             tot = rb[0]
             for k in range(1, N_BAND):
                 tot = tot + rb[k]
-            gs[...] = tot
-            gr[p] = tot
+            gs[...] = tot[0:2]
+            gr[p] = tot[0:2]
             proj = pr_ref[...]
             hp = lax.Precision.HIGHEST
-            u, w = nt(proj, qb[:, 0, :], precision=hp), nt(proj, qb[:, 1, :], precision=hp)
+            u, w = nt(proj, rb[:, 2, :], precision=hp), nt(proj, rb[:, 3, :], precision=hp)
             corr_ref[...] = jnp.concatenate([u[0:1] + w[1:2], w[0:1] - u[1:2]], axis=0)
 
         @pl.when(i == 8)
         def _():
-            each(1, N_PW, lambda s: grc(pw_peer(p, s), p).start())
+            each(1, N_PW, lambda s: copy(gs, gr.at[p], gr_s, gr_r, pw=pw_peer(p, s)).start())
     each(0, N_PW, backward)
 
     x, y, z = split_index(idx_ref[...])
@@ -392,33 +390,25 @@
     loc_ref[0] += kin * cf[:, 0, :]
     loc_ref[1] += kin * cf[:, 1, :]
 
-    each(1, N_PW, lambda s: grc(pw_peer(p, s), pw_peer(p, s)).wait_recv())
+    gr_all.wait_recv()
     tot = gr[0]
     for k in range(1, N_PW):
         tot = tot + gr[k]
-    g_out[...] = (tot[:, 0:48] + corr_ref[...]) * (1.0 / 98304.0)
+    g_out[...] = tot[:, 0:48] + corr_ref[...]
+
+    lr_all.wait_recv()
 
     def add_part(s):
-        src = pw_peer(p, 16 - s)
-        lrc(src, src).wait_recv()
-        loc_ref[...] += lr[src].astype(F32)
+        loc_ref[...] += lr[pw_peer(p, s)].astype(F32)
     each(1, N_PW, add_part)
     for t in range(48):
         sl = slice(128 * t, 128 * (t + 1))
         h = jnp.concatenate([loc_ref[0, t:t + 1, :], loc_ref[1, t:t + 1, :]], axis=0)
-        h_ref[:, sl] = (h + nl_ref[0:2, sl]).astype(BF16)
-
-    def drain_pw(s):
-        q = pw_peer(p, s)
-        for c in (agp, agi, pjc, grc, lrc):
-            c(q, p).wait_send()
-    each(1, N_PW, drain_pw)
-
-    def drain_band(s):
-        q = band_peer(s)
-        for c in (gbc, rbc, qbc):
-            c(q, b).wait_send()
-    each(1, N_BAND, drain_band)
+        h_ref[:, sl] = h + nl_ref[0:2, sl]
+
+    for sent in (all_of(ag_psi, N_PW - 1, agp_s, agp_r.at[0]), all_of(ag_idx, N_PW - 1, agi_s, agi_r.at[0]),
+                 pj_all, gb_all, rb_all, gr_all, lr_all):
+        sent.wait_send()
 
 
 def on_device(psi, gvec_index, vloc, beta, dmat, qmat):
@@ -432,8 +422,7 @@
     full = pl.BlockSpec(memory_space=vm)
     h, s, g = pl.pallas_call(
         kernel,
-        out_shape=(jax.ShapeDtypeStruct((2, 6144), BF16), jax.ShapeDtypeStruct((2, 6144), BF16),
-                   jax.ShapeDtypeStruct((2, 48), F32)),
+        out_shape=(jax.ShapeDtypeStruct((2, 6144), F32),) * 2 + (jax.ShapeDtypeStruct((2, 48), F32),),
         in_specs=[pl.BlockSpec(memory_space=pl.ANY)] * 10,
         out_specs=(full,) * 3,
         scratch_shapes=[
@@ -444,14 +433,15 @@
             vm((2352, 128), F32), vm((216, 256), F32), vm((776, 128), F32), vm((8, 6144), F32),
             vm((2, 48, 128), F32), vm((8, 128), F32),
             vm((16, 2, 48, 128), BF16), vm((16, 48, 128), jnp.int32), vm((8, 128), F32), vm((16, 8, 128), F32),
-            vm((48, 2, 128), F32), vm((48, 2, 128), F32), vm((48, 2, 128), F32), vm((48, 2, 128), F32),
-            vm((2, 128), F32), vm((48, 2, 128), F32), vm((2, 128), F32), vm((16, 2, 128), F32),
+            vm((48, 2, 128), F32), vm((48, 2, 128), F32), vm((48, 4, 128), F32), vm((48, 4, 128), F32),
+            vm((2, 128), F32), vm((16, 2, 128), F32),
             vm((16, 2, 48, 128), BF16), vm((16, 2, 48, 128), BF16),
-        ] + [dma((16,))] * 6 + [dma((48,))] * 6 + [dma((16,))] * 4,
+        ] + [dma((16,))] * 2 + [dma] * 12,
         compiler_params=pltpu.CompilerParams(collective_id=0, has_side_effects=True,
                                              vmem_limit_bytes=60 * 1024 * 1024),
     )(rows, idx, planes, beta, *mats, *tabs)
-    return h[:, None, :], s[:, None, :], g[:, None, :]
+    h, s = h.astype(BF16), s.astype(BF16)
+    return h[:, None, :], s[:, None, :], g[:, None, :] * (1.0 / 98304.0)
 
 
 def solution(mesh):

time: 101 us -> 92.2 us (0.913)
  Pallas kernels: 95.2 us -> 88 us
  local copies, waits for them, and re-layouts: 3.92 us -> 0 us
  other arithmetic: 0 us -> 2.7 us
    pallas_call x1, Pallas kernels: 95.2 us -> 88 us  [on_device(): pl.pallas_call(kernel, out_shape=(jax.ShapeDtypeStruct((2, 6144), F32),)...]
    unnamed x3 -> x0, local copies, waits for them, and re-layouts: 3.92 us -> none
    broadcast_in_dim x0 -> x1, other arithmetic: none -> 1.47 us  [on_device(): return (h[:, None, :], s[:, None, :], g[:, None, :] * (1.0 / 98304.0))]
    mul x0 -> x1, other arithmetic: none -> 1.22 us  [on_device(): return (h[:, None, :], s[:, None, :], g[:, None, :] * (1.0 / 98304.0))]
where the time goes in v2:
time: 92.2 us; the launch traced here: 91.3 us
  Pallas kernels  88 us (95%)
  other arithmetic  2.7 us (3%)
    pallas_call x1, Pallas kernels, on_device(): pl.pallas_call(kernel, out_shape=(jax.ShapeDtypeStruct((2, 6144), F32),)...  88 us

profile of v2, /device:TPU:1, one launch (start us, length us, event | category | flops | bytes accessed | tf_op | source)
XLA Modules:
  0.0 91.3 jit_solution(11425336105457337427)
XLA Ops:
  0.6 88.0 %shard_map.121 = (f32[2,6144]{1,0:T(2,128)}, f32[2,6144]{1,0:T(2,128)}, f32[2,48]{1,0:T(2,128)}) custom-call(bf16[2,6144]{1,0:T(2,128)(2,1)} %bitcast.15, s32[48,128]{1,0:T(8,128)} %bitcast.16, f32[12,192,192]{2,1,0:T(8,128)} %bitcast.12, bf16[2,72,6144]{2,1,0:T(8,128)(2,1)} %beta_hbm.1, f32[18,4,18]{2,1,0:T(4,128)} %bitcast.13, f32[18,4,18]{2,1,0:T(4,128)} %bitcast.14, ...), custom_call_target="tpu_custom_call" | custom-call | tf_op jit(solution)/shard_map/pallas_call | solution.py:423
  88.6 1.5 %convert_bitcast_fusion = (bf16[2,1,6144]{2,0,1:T(2,128)(2,1)}, bf16[2,1,6144]{2,0,1:T(2,128)(2,1)}) fusion(f32[2,6144]{1,0:T(2,128)} %get-tuple-element.7, f32[2,6144]{1,0:T(2,128)} %get-tuple-element.6), kind=kLoop, calls=%fused_computation | loop fusion | flops 24576 | bytes 147456 | tf_op jit(solution)/shard_map/broadcast_in_dim | solution.py:444
  90.1 1.2 %broadcast_multiply_fusion = f32[2,48]{1,0:T(2,128)} fusion(f32[2,48]{1,0:T(2,128)} %get-tuple-element.8), kind=kLoop, calls=%fused_computation.2 | loop fusion | flops 96 | bytes 768 | tf_op jit(solution)/shard_map/mul | solution.py:444

commit v3 on v2

--- a/solution.py
+++ b/solution.py
@@ -234,7 +234,7 @@
     loads = [pltpu.make_async_copy(src, dst, in_sem.at[k]) for k, (src, dst) in enumerate((
         (psi_hbm, psi_ref), (idx_hbm, idx_ref), (beta_hbm, beta_ref), (d_hbm, d_ref), (q_hbm, q_ref),
         (vloc_hbm, vloc_ref), (zp_hbm, zp), (zm_hbm, zm), (xp_hbm, xp), (xm_hbm, xm)))]
-    for load in loads:
+    for load in loads[:3]:
         load.start()
     barrier = pltpu.get_barrier_semaphore()
     each(1, N_PW, lambda s: pl.semaphore_signal(barrier, inc=1, device_id={"pw": pw_peer(p, s)},
@@ -242,6 +242,8 @@
     each(1, N_BAND, lambda s: pl.semaphore_signal(barrier, inc=1, device_id={"band": band_peer(s)},
                                                   device_id_type=pl.DeviceIdType.MESH))
 
+    for load in loads[3:]:
+        load.start()
     loads[0].wait()
     loads[1].wait()
     for t in range(48):
@@ -271,6 +273,13 @@
     pj_send[1:2, 0:72] = pr[1:2] - pi[0:1]
     pj_recv[p] = pj_send[...]
     m_ref[...] = jnp.zeros_like(m_ref)
+    for k in range(3, 5):
+        loads[k].wait()
+    bd_ref[...] = jnp.zeros_like(bd_ref)
+    for a in range(4):
+        sl = slice(18 * a, 18 * a + 18)
+        bd_ref[0, sl, sl] = d_ref[:, a, :]
+        bd_ref[1, sl, sl] = q_ref[:, a, :]
 
     def start_first(s):
         q = pw_peer(p, s)
@@ -316,13 +325,8 @@
     for k in range(1, N_PW):
         proj = proj + pj_recv[k]
     pr_ref[...] = proj
-    for k in range(3, 10):
+    for k in range(5, 10):
         loads[k].wait()
-    bd_ref[...] = jnp.zeros_like(bd_ref)
-    for a in range(4):
-        sl = slice(18 * a, 18 * a + 18)
-        bd_ref[0, sl, sl] = d_ref[:, a, :]
-        bd_ref[1, sl, sl] = q_ref[:, a, :]
     dc = nt(proj, bd_ref[0], precision=lax.Precision.HIGHEST)
     qc = nt(proj, bd_ref[1], precision=lax.Precision.HIGHEST)
     qc = qc.astype(BF16).astype(F32)

time: 92.2 us -> 92.1 us (level)
  no operation moved by 1% of the time
where the time goes in v3:
time: 92.1 us; the launch traced here: 91.2 us
  Pallas kernels  87.8 us (95%)
  other arithmetic  2.7 us (3%)
    pallas_call x1, Pallas kernels, on_device(): pl.pallas_call(kernel, out_shape=(jax.ShapeDtypeStruct((2, 6144), F32),)...  87.8 us

profile of v3, /device:TPU:1, one launch (start us, length us, event | category | flops | bytes accessed | tf_op | source)
XLA Modules:
  0.0 91.2 jit_solution(16337293871283868091)
XLA Ops:
  0.6 87.8 %shard_map.121 = (f32[2,6144]{1,0:T(2,128)}, f32[2,6144]{1,0:T(2,128)}, f32[2,48]{1,0:T(2,128)}) custom-call(bf16[2,6144]{1,0:T(2,128)(2,1)} %bitcast.15, s32[48,128]{1,0:T(8,128)} %bitcast.16, f32[12,192,192]{2,1,0:T(8,128)} %bitcast.12, bf16[2,72,6144]{2,1,0:T(8,128)(2,1)} %beta_hbm.1, f32[18,4,18]{2,1,0:T(4,128)} %bitcast.13, f32[18,4,18]{2,1,0:T(4,128)} %bitcast.14, ...), custom_call_target="tpu_custom_call" | custom-call | tf_op jit(solution)/shard_map/pallas_call | solution.py:427
  88.5 1.5 %convert_bitcast_fusion = (bf16[2,1,6144]{2,0,1:T(2,128)(2,1)}, bf16[2,1,6144]{2,0,1:T(2,128)(2,1)}) fusion(f32[2,6144]{1,0:T(2,128)} %get-tuple-element.7, f32[2,6144]{1,0:T(2,128)} %get-tuple-element.6), kind=kLoop, calls=%fused_computation | loop fusion | flops 24576 | bytes 147456 | tf_op jit(solution)/shard_map/broadcast_in_dim | solution.py:448
  90.0 1.2 %broadcast_multiply_fusion = f32[2,48]{1,0:T(2,128)} fusion(f32[2,48]{1,0:T(2,128)} %get-tuple-element.8), kind=kLoop, calls=%fused_computation.2 | loop fusion | flops 96 | bytes 768 | tf_op jit(solution)/shard_map/mul | solution.py:448
